TPU v7x, 256 devices: a whole 4x4x8 slice. The times are simulated.
256 devices in a mesh: seq: 64 (over y, z, core), tp: 4 (over x).
Axes of the slice: x: 4, y: 4, z: 8, core: 2. Of those that a mesh axis runs over, the one named last changes fastest.
Arguments:
- stream: bfloat16 [8192, 2048], P('seq'), may hold values from -256 to 256
- lengths: int32 [6], replicated, may hold values from 1 to 7168, 8192 in all
- q_weight: bfloat16 [2048, 1536], P(None, 'tp'), may hold values from -0.125 to 0.125
- kv_down: bfloat16 [2048, 576], replicated, may hold values from -0.125 to 0.125
- latent_gain: float32 [512], replicated, may hold values from 0.1 to 1.9
- kv_up: bfloat16 [8, 512, 256], P('tp'), may hold values from -0.25 to 0.25
- out_weight: bfloat16 [1024, 2048], P('tp'), may hold values from -0.1875 to 0.1875
- moe_gain: float32 [2048], replicated, may hold values from 0.1 to 1.9
- routes: int32 [8192, 6], P('seq'), may hold values from 0 to 63, all different within a row; in each aligned block of 128 rows (0 to 127, 128 to 255, ...) at most 24 rows name the same one
- route_weight: float32 [8192, 6], P('seq'), may hold values from 0.05 to 0.5
- expert_gate: bfloat16 [64, 2048, 1408], P('seq', None, 'tp'), may hold values from -0.125 to 0.125
- expert_up: bfloat16 [64, 2048, 1408], P('seq', None, 'tp'), may hold values from -0.125 to 0.125
- expert_down: bfloat16 [64, 1408, 2048], P('seq', 'tp'), may hold values from -0.15625 to 0.15625
Outputs:
- layer_out: bfloat16 [8192, 2048], P('seq')
- latent_cache: bfloat16 [8192, 576], P('seq')
Inputs may be any that keep to these rules, and one draw needn't show every extreme that they name: 6 lengths summing to 8192, the longest exactly 7168. In each aligned block of 128 rows no expert is named by more than 24 routes, a bound that some block reaches.
All inputs are finite; a program needn't handle non-finite values.
Results may differ from a plain program's by a relative error of at most 0.0075.
Values may be sent and summed in bfloat16 or wider, within the bound.
A program may use at most 128 MiB of HBM per device.

v0:
```python
import jax
import jax.numpy as jnp
from jax import lax
from jax.sharding import PartitionSpec as P

D = 2048
NOPE = 128
ROPE = 64
LATENT = 512
VDIM = 128
THETA = 50000.0


def place(token_index, lengths):
    prompt_ends = jnp.cumsum(lengths)
    before = (prompt_ends[None, :] <= token_index[:, None]).astype(jnp.int32)
    segment = jnp.sum(before, axis=1)
    prompt_start = jnp.sum(before * lengths[None, :], axis=1)
    return (segment, token_index - prompt_start)


def angles(position):
    half_rope = ROPE // 2
    frequency = THETA ** (-2.0 * jnp.arange(half_rope, dtype=jnp.float32) / ROPE)
    angle_table = position.astype(jnp.float32)[:, None] * frequency[None, :]
    return (jnp.cos(angle_table), jnp.sin(angle_table))


def rotate(values, cos_table, sin_table):
    half_rope = ROPE // 2
    first_half = values[..., :half_rope]
    second = values[..., half_rope:]
    return jnp.concatenate(
        [first_half * cos_table - second * sin_table, first_half * sin_table + second * cos_table],
        axis=-1,
    )


def on_device(
    stream,
    lengths,
    q_weight,
    kv_down,
    latent_gain,
    kv_up,
    out_weight,
    moe_gain,
    routes,
    route_weight,
    expert_gate,
    expert_up,
    expert_down,
):
    tok_count = stream.shape[0]
    head_count = kv_up.shape[0]
    first_row = lax.axis_index("seq") * tok_count
    token_index = first_row + jnp.arange(tok_count, dtype=jnp.int32)
    segment, position = place(token_index, lengths)
    cos_table, sin_table = angles(position)
    kv_proj = jnp.dot(stream, kv_down, preferred_element_type=jnp.float32)
    compressed = kv_proj[:, :LATENT]
    factor = lax.rsqrt(jnp.mean(compressed * compressed, axis=1, keepdims=True) + 1e-06)
    latent = jnp.concatenate(
        [
            compressed * factor * latent_gain[None, :],
            rotate(kv_proj[:, LATENT:], cos_table, sin_table),
        ],
        axis=1,
    ).astype(jnp.bfloat16)
    tp_count = lax.axis_size("tp")
    tp_index = lax.axis_index("tp")
    kv_up_all = lax.all_gather(kv_up, "tp", axis=0, tiled=True)
    all_heads = kv_up_all.shape[0]
    q_proj = jnp.dot(stream, q_weight, preferred_element_type=jnp.float32).astype(jnp.bfloat16)
    q_proj = lax.all_gather(q_proj, "tp", axis=1, tiled=True)
    q_proj = q_proj.reshape(tok_count, all_heads, NOPE + ROPE)
    absorbed = jnp.einsum(
        "thj,hcj->thc",
        q_proj[:, :, :NOPE],
        kv_up_all[:, :, :NOPE],
        preferred_element_type=jnp.float32,
    )
    rotated = rotate(
        q_proj[:, :, NOPE:].astype(jnp.float32), cos_table[:, None, :], sin_table[:, None, :]
    )
    softmax_scale = (NOPE + ROPE) ** (-0.5)
    queries = (jnp.concatenate([absorbed, rotated], axis=2) * softmax_scale).astype(jnp.bfloat16)
    queries = queries.reshape(tok_count * all_heads, LATENT + ROPE)
    row_segment = jnp.repeat(segment, all_heads)
    row_index = jnp.repeat(token_index, all_heads)
    key_rows = tok_count // tp_count
    own_keys = lax.dynamic_slice_in_dim(latent, tp_index * key_rows, key_rows, 0)
    shard_rows = lax.all_gather(own_keys, "seq", axis=0, tiled=True)
    seq_count = shard_rows.shape[0] // key_rows
    key_index = (
        jnp.arange(seq_count, dtype=jnp.int32)[:, None] * tok_count
        + tp_index * key_rows
        + jnp.arange(key_rows, dtype=jnp.int32)[None, :]
    ).reshape(-1)
    key_segment, unused = place(key_index, lengths)
    allowed = (row_segment[:, None] == key_segment[None, :]) & (
        key_index[None, :] <= row_index[:, None]
    )
    scores = jnp.einsum("ra,ka->rk", queries, shard_rows, preferred_element_type=jnp.float32)
    block_peak = jnp.max(jnp.where(allowed, scores, -jnp.inf), axis=1)
    peak = jnp.maximum(jnp.full_like(block_peak, -1e30), block_peak)
    weights = jnp.where(allowed, jnp.exp(scores - peak[:, None]), 0.0)
    weight_sum = jnp.sum(weights, axis=1)
    context_sum = jnp.dot(
        weights.astype(jnp.bfloat16), shard_rows[:, :LATENT], preferred_element_type=jnp.float32
    ).reshape(tok_count, all_heads, LATENT)
    heads_part = jnp.einsum(
        "thc,hcv->thv",
        context_sum,
        kv_up_all[:, :, NOPE:].astype(jnp.float32),
        precision=lax.Precision.HIGHEST,
    )
    packed = jnp.concatenate(
        [
            heads_part,
            weight_sum.reshape(tok_count, all_heads, 1),
            peak.reshape(tok_count, all_heads, 1),
        ],
        axis=2,
    )
    packed = packed.reshape(tok_count, tp_count, head_count, VDIM + 2).transpose(1, 0, 2, 3)
    packed = lax.all_to_all(packed, "tp", split_axis=0, concat_axis=0, tiled=True)
    part_peak = packed[:, :, :, VDIM + 1]
    top_peak = jnp.max(part_peak, axis=0)
    rescale = jnp.exp(part_peak - top_peak[None])
    numerator = jnp.sum(packed[:, :, :, :VDIM] * rescale[..., None], axis=0)
    denominator = jnp.sum(packed[:, :, :, VDIM] * rescale, axis=0)
    heads_out = numerator / denominator[..., None]
    heads_out = heads_out.astype(jnp.bfloat16).reshape(tok_count, head_count * VDIM)
    partial_attention = jnp.dot(heads_out, out_weight, preferred_element_type=jnp.float32)
    tp_count = lax.axis_size("tp")
    col_width = D // tp_count
    col_start = lax.axis_index("tp") * col_width
    attention_part = lax.psum_scatter(
        partial_attention.astype(jnp.bfloat16), "tp", scatter_dimension=1, tiled=True
    ).astype(jnp.float32)
    stream_part = lax.dynamic_slice_in_dim(stream, col_start, col_width, 1)
    hidden = stream_part.astype(jnp.float32) + attention_part
    square_sum = lax.psum(jnp.sum(hidden * hidden, axis=1, keepdims=True), "tp")
    gain_part = lax.dynamic_slice_in_dim(moe_gain, col_start, col_width, 0)
    normed = (hidden * lax.rsqrt(square_sum / D + 1e-06) * gain_part[None, :]).astype(jnp.bfloat16)
    experts = lax.axis_size("seq")
    top_k = routes.shape[1]
    capacity = min(tok_count, max(2, 2 * tok_count * top_k // experts))
    flat_routes = routes.reshape(-1)
    onehot = (flat_routes[:, None] == jnp.arange(experts, dtype=jnp.int32)[None, :]).astype(
        jnp.int32
    )
    slot_rank = jnp.sum((jnp.cumsum(onehot, axis=0) - onehot) * onehot, axis=1)
    slot_index = flat_routes * capacity + slot_rank
    slot_table = (
        slot_index[:, None] == jnp.arange(experts * capacity, dtype=jnp.int32)[None, :]
    ).astype(jnp.bfloat16)
    placing = jnp.sum(slot_table.reshape(tok_count, top_k, experts * capacity), axis=1)
    outgoing = jnp.einsum("ts,td->sd", placing, normed, preferred_element_type=jnp.float32).astype(
        jnp.bfloat16
    )
    outgoing = outgoing.reshape(experts, capacity, col_width)
    chunk_count = 2
    chunk_slots = capacity // chunk_count
    returned_chunks = []
    for chunk in range(chunk_count):
        sending = outgoing[:, chunk * chunk_slots : (chunk + 1) * chunk_slots]
        received = lax.all_to_all(sending, "seq", split_axis=0, concat_axis=0, tiled=True)
        sources, slot_count, _ = received.shape
        flat_part = received.reshape(sources * slot_count, col_width)
        flat_rows = lax.all_gather(flat_part, "tp", axis=1, tiled=True)
        gate_act = jnp.dot(flat_rows, expert_gate[0], preferred_element_type=jnp.float32)
        up_act = jnp.dot(flat_rows, expert_up[0], preferred_element_type=jnp.float32)
        hidden_units = (jax.nn.silu(gate_act) * up_act).astype(jnp.bfloat16)
        expert_out = jnp.dot(
            hidden_units, expert_down[0], preferred_element_type=jnp.float32
        ).astype(jnp.bfloat16)
        expert_sum = lax.psum_scatter(expert_out, "tp", scatter_dimension=1, tiled=True)
        expert_sum = expert_sum.reshape(sources, slot_count, col_width)
        returned_chunks.append(
            lax.all_to_all(expert_sum, "seq", split_axis=0, concat_axis=0, tiled=True)
        )
    returned = jnp.concatenate(returned_chunks, axis=1)
    gathered = returned.reshape(experts * capacity, col_width)[slot_index].reshape(
        tok_count, top_k, col_width
    )
    moe = jnp.zeros((tok_count, col_width), jnp.float32)
    for route_slot in range(top_k):
        moe = moe + route_weight[:, route_slot][:, None] * gathered[:, route_slot].astype(
            jnp.float32
        )
    layer_part = (hidden + moe).astype(jnp.bfloat16)
    layer_out = lax.all_gather(layer_part, "tp", axis=1, tiled=True)
    return (layer_out, latent)


def solution(mesh):
    return jax.shard_map(
        on_device,
        mesh=mesh,
        in_specs=(
            P("seq", None),
            P(),
            P(None, "tp"),
            P(),
            P(),
            P("tp", None, None),
            P("tp", None),
            P(),
            P("seq", None),
            P("seq", None),
            P("seq", None, "tp"),
            P("seq", None, "tp"),
            P("seq", "tp", None),
        ),
        out_specs=(P("seq", None), P("seq", None)),
        check_vma=False,
    )
```

profile of v0, /device:TPU:32, one launch (start us, length us, event | category | flops | bytes accessed | tf_op | source)
XLA Modules:
  0.0 472.8 jit_solution(8885224359928597981)
XLA Ops:
  9.6 1.9 fusion.82
  12.9 1.8 convolution_convert_fusion.4
  14.7 13.1 %all_gather.18 = bf16[128,1536]{1,0:T(8,128)(2,1)S(1)} all-gather(bf16[128,384]{1,0:T(8,128)(2,1)S(1)} %convolution_convert_fusion.4), channel_id=1, replica_groups=mesh['seq'=64,'tp'=4] {'tp'}, dimensions={1}, use_global_device_ids=true | all-gather | bytes 491520 | tf_op jit(solution)/shard_map/all_gather | solution.py:75
  30.7 15.1 %all-gather.5.cloned.1.call-done = bf16[8,512,256]{2,1,0:T(8,128)(2,1)} async-done(((bf16[2,512,256]{2,1,0:T(8,128)(2,1)}), bf16[8,512,256]{2,1,0:T(8,128)(2,1)}) %all-gather.5.cloned.1.call-update) | async-done | bytes 2097168 | tf_op jit(solution)/shard_map/all_gather | solution.py:72
  47.5 2.5 copy.143
  50.0 75.5 %all-gather.7.cloned.1.call-done = bf16[2048,576]{1,0:T(8,128)(2,1)} async-done(((bf16[32,576]{1,0:T(8,128)(2,1)}), bf16[2048,576]{1,0:T(8,128)(2,1)}) %all-gather.7.cloned.1.call-update) | async-done | bytes 2359312 | tf_op jit(solution)/shard_map/all_gather | solution.py:93
  125.5 8.6 %select_reduce_fusion = (f32[1024]{0:T(1024)S(1)}, f32[1024,2048]{1,0:T(8,128)}) fusion(s32[2048]{0:T(1024)S(1)} %add.144, s32[2048]{0:T(1024)S(1)} %convert_reduce_fusion, s32[1024]{0:T(1024)S(1)} %le.48, s32[1024]{0:T(1024)S(1)} %eq.54, bf16[2048,576]{1,0:T(8,128)(2,1)} %all-gather.7.cloned.1.call-done, f32[1024,32]{1,0:T(8,128)} %bitcast.153, ...), kind=kOutput, calls=%fused_computation.2 | convolution fusion | flops 2428763136 | bytes 13135872 | tf_op jit(solution)/shard_map/ra,ka->rk/dot_general | solution.py:104
  134.4 5.5 %fusion = f32[1024]{0:T(1024)S(1)} fusion(f32[1024,2048]{1,0:T(8,128)} %get-tuple-element.29, f32[1024]{0:T(1024)S(1)} %broadcast_maximum_fusion, s32[2048]{0:T(1024)S(1)} %add.144, s32[2048]{0:T(1024)S(1)} %convert_reduce_fusion, s32[1024]{0:T(1024)S(1)} %le.48, s32[1024]{0:T(1024)S(1)} %eq.54), kind=kLoop, calls=%fused_computation.4 | loop fusion | flops 12581888 | bytes 8421376 | tf_op jit(solution)/shard_map/reduce_sum | solution.py:108
  140.2 4.3 fusion.10
  144.5 2.4 fusion.8
  148.2 14.0 %all_to_all.25 = f32[4,128,2,130]{1,2,3,0:T(2,128)S(1)} all-to-all(f32[4,128,2,130]{1,2,3,0:T(2,128)S(1)} %maximum_bitcast_fusion), channel_id=1, replica_groups=mesh['seq'=64,'tp'=4] {'tp'}, dimensions={0} | all-to-all | bytes 1064960 | tf_op jit(solution)/shard_map/all_to_all | solution.py:127
  164.2 2.0 reduce-window.19
  168.3 16.3 %reduce-scatter.4.cloned.1.call-done = bf16[128,512]{1,0:T(8,128)(2,1)} async-done(((bf16[128,2048]{1,0:T(8,128)(2,1)}), bf16[128,512]{1,0:T(8,128)(2,1)}) %reduce-scatter.4.cloned.1.call-update) | async-done | bytes 131088 | tf_op jit(solution)/shard_map/reduce_scatter | solution.py:139
  185.7 8.4 %psum.7 = f32[128,1]{0,1:T(1,128)S(1)} all-reduce(f32[128,1]{0,1:T(1,128)S(1)} %bitcast.158), channel_id=1, replica_groups=mesh['seq'=64,'tp'=4] {'tp'}, use_global_device_ids=true, to_apply=%region_16.17 | all-reduce | flops 128 | bytes 1024 | tf_op jit(solution)/shard_map/psum | solution.py:144
  196.0 38.2 %all_to_all.26 = bf16[64,12,512]{2,1,0:T(8,128)(2,1)S(1)} all-to-all(bf16[64,12,512]{2,1,0:T(8,128)(2,1)S(1)} %get-tuple-element.4), channel_id=1, replica_groups=mesh['seq'=64,'tp'=4] {'seq'}, dimensions={0} | all-to-all | bytes 1572864 | tf_op jit(solution)/shard_map/all_to_all | solution.py:169
  235.3 34.5 %all_to_all.27 = bf16[64,12,512]{2,1,0:T(8,128)(2,1)S(1)} all-to-all(bf16[64,12,512]{2,1,0:T(8,128)(2,1)S(1)} %get-tuple-element.5), channel_id=1, replica_groups=mesh['seq'=64,'tp'=4] {'seq'}, dimensions={0} | all-to-all | bytes 1572864 | tf_op jit(solution)/shard_map/all_to_all | solution.py:169
  271.0 2.5 all-gather.9.cloned.1.call-done
  273.5 3.6 fusion.23
  277.2 7.8 %convolution_convert_fusion.1 = bf16[768,2048]{1,0:T(8,128)(2,1)} fusion(bf16[1,352,2048]{2,1,0:T(8,128)(2,1)S(1)} %copy-done.15, bf16[768,2048]{1,0:T(8,128)(2,1)} %all-gather.9.cloned.1.call-done, bf16[1,2048,352]{1,2,0:T(8,128)(2,1)} %param.24, f32[768,352]{0,1:T(8,128)S(1)} %fusion.23), kind=kOutput, calls=%fused_computation.10 | convolution fusion | flops 2217787392 | bytes 10256384 | tf_op jit(solution)/shard_map/dot_general | solution.py:176
  285.3 32.2 %all-gather.11.cloned.1.call-done = bf16[768,2048]{1,0:T(8,128)(2,1)} async-done(((bf16[768,512]{1,0:T(8,128)(2,1)}), bf16[768,2048]{1,0:T(8,128)(2,1)}) %all-gather.11.cloned.1.call-update) | async-done | bytes 3145744 | tf_op jit(solution)/shard_map/all_gather | solution.py:172
  317.4 3.2 fusion.21
  320.6 8.2 %convolution_convert_fusion = bf16[768,2048]{1,0:T(8,128)(2,1)} fusion(bf16[1,352,2048]{2,1,0:T(8,128)(2,1)} %param.25, bf16[768,2048]{1,0:T(8,128)(2,1)} %all-gather.11.cloned.1.call-done, bf16[1,2048,352]{1,2,0:T(8,128)(2,1)} %param.24, f32[768,352]{0,1:T(8,128)S(1)} %fusion.21), kind=kOutput, calls=%fused_computation.9 | convolution fusion | flops 2217787392 | bytes 10256384 | tf_op jit(solution)/shard_map/dot_general | solution.py:176
  328.9 32.0 %reduce-scatter.6.cloned.1.call-done = bf16[768,512]{1,0:T(8,128)(2,1)} async-done(((bf16[768,2048]{1,0:T(8,128)(2,1)}), bf16[768,512]{1,0:T(8,128)(2,1)}) %reduce-scatter.6.cloned.1.call-update) | async-done | bytes 786448 | tf_op jit(solution)/shard_map/reduce_scatter | solution.py:179
  360.9 2.2 reshape.278
  363.1 10.5 %all-to-all-start.2 = ((bf16[64,12,512]{2,1,0:T(8,128)(2,1)}), bf16[64,12,512]{2,1,0:T(8,128)(2,1)S(1)}, u32[]{:S(2)}, u32[]{:S(2)}) async-start(bf16[64,12,512]{2,1,0:T(8,128)(2,1)} %reshape.278), calls=%async_computation.4 | async-start | bytes 2097152 | tf_op jit(solution)/shard_map/all_to_all | solution.py:182
  373.6 30.5 %reduce-scatter.8.cloned.1.call-done = bf16[768,512]{1,0:T(8,128)(2,1)} async-done(((bf16[768,2048]{1,0:T(8,128)(2,1)}), bf16[768,512]{1,0:T(8,128)(2,1)}) %reduce-scatter.8.cloned.1.call-update) | async-done | bytes 786448 | tf_op jit(solution)/shard_map/reduce_scatter | solution.py:179
  404.1 2.1 reshape.280
  406.2 10.7 %all-to-all-start.4 = ((bf16[64,12,512]{2,1,0:T(8,128)(2,1)}), bf16[64,12,512]{2,1,0:T(8,128)(2,1)}, u32[]{:S(2)}, u32[]{:S(2)}) async-start(bf16[64,12,512]{2,1,0:T(8,128)(2,1)} %reshape.280), calls=%async_computation.7 | async-start | bytes 2097152 | tf_op jit(solution)/shard_map/all_to_all | solution.py:182
  417.6 27.1 %all-to-all-done.4 = bf16[64,12,512]{2,1,0:T(8,128)(2,1)} async-done(((bf16[64,12,512]{2,1,0:T(8,128)(2,1)}), bf16[64,12,512]{2,1,0:T(8,128)(2,1)}, u32[]{:S(2)}, u32[]{:S(2)}) %all-to-all-start.4) | async-done | bytes 786464 | tf_op jit(solution)/shard_map/all_to_all | solution.py:182
  444.7 1.7 pad_maximum_fusion
  446.4 2.7 gather_fusion
  451.7 13.4 %all_gather.23 = bf16[128,2048]{1,0:T(8,128)(2,1)S(1)} all-gather(bf16[128,512]{1,0:T(8,128)(2,1)S(1)} %fusion.52), channel_id=1, replica_groups=mesh['seq'=64,'tp'=4] {'tp'}, dimensions={1}, use_global_device_ids=true | all-gather | bytes 655360 | tf_op jit(solution)/shard_map/all_gather | solution.py:194
  (112 shorter events, 23.8 us)
Async XLA Ops:
  7.2 2.4 copy-start
  7.2 4.5 copy-start.11
  7.2 38.6 %all-gather.5.cloned.1.call-start = ((), (), s32[]{:S(2)}) async-start(), calls=%async_computation.8 | async-start | bytes 2621440 | tf_op jit(solution)/shard_map/all_gather | solution.py:72
  7.9 117.6 %all-gather.7.cloned.1.call-start = ((), (), s32[]{:S(2)}) async-start(), calls=%async_computation.9 | async-start | bytes 2662400 | tf_op jit(solution)/shard_map/all_gather | solution.py:93
  9.6 3.3 copy-start.3
  11.9 0.9 copy-start.7
  12.8 171.8 %reduce-scatter.4.cloned.1.call-start = ((), (), s32[]{:S(2)}) async-start(), calls=%async_computation.10 | async-start | bytes 655360 | tf_op jit(solution)/shard_map/reduce_scatter | solution.py:139
  47.5 78.0 %copy-start.8 = (f32[128,8,32]{2,1,0:T(8,128)S(1)}, f32[128,8,32]{2,1,0:T(8,128)}, u32[]{:S(2)}) copy-start(f32[128,8,32]{2,1,0:T(8,128)} %copy.86) | copy-start | bytes 393220
  134.4 5.8 %copy-start.2 = (f32[1024,2048]{1,0:T(8,128)S(1)}, f32[1024,2048]{1,0:T(8,128)}, u32[]{:S(2)}) copy-start(f32[1024,2048]{1,0:T(8,128)} %get-tuple-element.29) | copy-start | bytes 25165828
  140.2 4.3 copy-start.4
  147.3 15.2 %copy-start.6 = (bf16[256,2048]{1,0:T(8,128)(2,1)S(1)}, bf16[256,2048]{1,0:T(8,128)(2,1)}, u32[]{:S(2)}) copy-start(bf16[256,2048]{1,0:T(8,128)(2,1)} %param.19) | copy-start | bytes 3145732
  148.2 15.6 %copy-start.9 = (s32[128,6]{0,1:T(8,128)S(1)}, s32[128,6]{0,1:T(8,128)}, u32[]{:S(2)}) copy-start(s32[128,6]{0,1:T(8,128)} %param.21) | copy-start | bytes 9220
  163.7 109.8 %all-gather.9.cloned.1.call-start = ((), (), s32[]{:S(2)}) async-start(), calls=%async_computation.11 | async-start | bytes 3932160 | tf_op jit(solution)/shard_map/all_gather | solution.py:172
  235.3 82.1 %all-gather.11.cloned.1.call-start = ((), (), s32[]{:S(2)}) async-start(), calls=%async_computation.13 | async-start | bytes 3932160 | tf_op jit(solution)/shard_map/all_gather | solution.py:172
  271.0 6.2 %copy-start.15 = (bf16[1,352,2048]{2,1,0:T(8,128)(2,1)S(1)}, bf16[1,352,2048]{2,1,0:T(8,128)(2,1)}, u32[]{:S(2)}) copy-start(bf16[1,352,2048]{2,1,0:T(8,128)(2,1)} %param.25) | copy-start | bytes 4325380
  271.0 89.9 %reduce-scatter.6.cloned.1.call-start = ((), (), s32[]{:S(2)}) async-start(), calls=%async_computation.12 | async-start | bytes 3932160 | tf_op jit(solution)/shard_map/reduce_scatter | solution.py:179
  284.9 32.5 %copy-start.14 = (bf16[1,2048,352]{1,2,0:T(8,128)(2,1)S(1)}, bf16[1,2048,352]{1,2,0:T(8,128)(2,1)}, u32[]{:S(2)}) copy-start(bf16[1,2048,352]{1,2,0:T(8,128)(2,1)} %param.23) | copy-start | bytes 4325380
  284.9 119.1 %reduce-scatter.8.cloned.1.call-start = ((), (), s32[]{:S(2)}) async-start(), calls=%async_computation.14 | async-start | bytes 3932160 | tf_op jit(solution)/shard_map/reduce_scatter | solution.py:179
  363.1 43.1 %all-to-all-start.2 = ((bf16[64,12,512]{2,1,0:T(8,128)(2,1)}), bf16[64,12,512]{2,1,0:T(8,128)(2,1)S(1)}, u32[]{:S(2)}, u32[]{:S(2)}) async-start(bf16[64,12,512]{2,1,0:T(8,128)(2,1)} %reshape.278), calls=%async_computation.4 | async-start | bytes 2097152 | tf_op jit(solution)/shard_map/all_to_all | solution.py:182
  373.6 43.5 %copy-start.10 = (f32[128,6]{0,1:T(8,128)S(1)}, f32[128,6]{0,1:T(8,128)}, u32[]{:S(2)}) copy-start(f32[128,6]{0,1:T(8,128)} %param.22) | copy-start | bytes 9220
  406.2 38.5 %all-to-all-start.4 = ((bf16[64,12,512]{2,1,0:T(8,128)(2,1)}), bf16[64,12,512]{2,1,0:T(8,128)(2,1)}, u32[]{:S(2)}, u32[]{:S(2)}) async-start(bf16[64,12,512]{2,1,0:T(8,128)(2,1)} %reshape.280), calls=%async_computation.7 | async-start | bytes 2097152 | tf_op jit(solution)/shard_map/all_to_all | solution.py:182
  449.1 1.5 copy-start.5
  449.3 1.2 copy-start.12
  449.4 1.2 copy-start.13
  449.4 16.6 %copy-start.1 = (bf16[2048,576]{0,1:T(8,128)(2,1)S(1)}, bf16[2048,576]{0,1:T(8,128)(2,1)}, u32[]{:S(2)}) copy-start(bf16[2048,576]{0,1:T(8,128)(2,1)} %param.16) | copy-start | bytes 7077892
Sparse Core Ops, SparseCore 0:
  9.8 35.8 all-gather.4
  48.5 76.9 all-gather.6
  163.8 20.7 reduce-scatter.3
  235.4 38.0 all-gather.8
  275.2 42.2 all-gather.10
  319.8 41.0 reduce-scatter.5
  363.5 40.5 reduce-scatter.7
where the time goes:
time: 474 us; the launch traced here: 473 us
  waiting for transfers between devices  232 us (49%)
  blocking collectives  122 us (26%)
  matrix products  46.1 us (10%)
  local copies, waits for them, and re-layouts  21.8 us (5%)
  starting transfers between devices  21.7 us (5%)
  other arithmetic  15.1 us (3%)
  between operations  14.7 us (3%)
    all_gather x1, waiting for transfers between devices, on_device(): shard_rows = lax.all_gather(own_keys, 'seq', axis=0, tiled=True)  75.5 us
    all_to_all x2, blocking collectives, on_device(): lax.all_to_all(sending, 'seq', split_axis=0, concat_axis=0, tiled=True)  72.7 us
    reduce_scatter x2, waiting for transfers between devices, on_device(): lax.psum_scatter(expert_out, 'tp', scatter_dimension=1, tiled=True)  62.5 us
    all_gather x2, waiting for transfers between devices, on_device(): flat_rows = lax.all_gather(flat_part, 'tp', axis=1, tiled=True)  34.6 us
    all_to_all x2, waiting for transfers between devices, on_device(): lax.all_to_all(expert_sum, 'seq', split_axis=0, concat_axis=0, tiled=True)  27.1 us
    all_to_all x2, starting transfers between devices, on_device(): lax.all_to_all(expert_sum, 'seq', split_axis=0, concat_axis=0, tiled=True)  21.2 us
    reduce_scatter x1, waiting for transfers between devices, on_device(): lax.psum_scatter(partial_attention.astype(jnp.bfloat16), 'tp', scatter_di...  16.3 us
    dot_general x2, matrix products, on_device(): jnp.dot(hidden_units, expert_down[0], preferred_element_type=jnp.float32)  16 us
  transfers between devices with their start and end apart: 9, of which 8 were waited for; matrix products, arithmetic and copies ran while one was open for 10% of the time, Pallas kernels for 0%

commit v1 on v0

--- a/solution.py
+++ b/solution.py
@@ -169,7 +169,9 @@
         received = lax.all_to_all(sending, "seq", split_axis=0, concat_axis=0, tiled=True)
         sources, slot_count, _ = received.shape
         flat_part = received.reshape(sources * slot_count, col_width)
-        flat_rows = lax.all_gather(flat_part, "tp", axis=1, tiled=True)
+        flat_rows = jnp.concatenate(
+            lax.all_to_all(jnp.stack([flat_part] * lax.axis_size("tp")), "tp", 0, 0), axis=1
+        )
         gate_act = jnp.dot(flat_rows, expert_gate[0], preferred_element_type=jnp.float32)
         up_act = jnp.dot(flat_rows, expert_up[0], preferred_element_type=jnp.float32)
         hidden_units = (jax.nn.silu(gate_act) * up_act).astype(jnp.bfloat16)

time: 474 us -> 487 us (1.027)
  blocking collectives: 122 us -> 205 us
  waiting for transfers between devices: 232 us -> 162 us
    all_to_all x0 -> x2, blocking collectives: none -> 83.1 us  [on_device(): lax.all_to_all(jnp.stack([flat_part] * lax.axis_size('tp')), 'tp', 0, 0)]
    reduce_scatter x2, waiting for transfers between devices: 62.5 us -> 27.8 us  [on_device(): lax.psum_scatter(expert_out, 'tp', scatter_dimension=1, tiled=True)]
    all_gather x2 -> x0, waiting for transfers between devices: 34.6 us -> none  [on_device(): flat_rows = lax.all_gather(flat_part, 'tp', axis=1, tiled=True)]
  transfers between devices with their start and end apart: 9 -> 7, of which waited for: 8 -> 5; matrix products, arithmetic and copies ran while one was open for 10% -> 7% of each run, Pallas kernels for 0% -> 0%
where the time goes in v1:
time: 487 us; the launch traced here: 483 us
  blocking collectives  205 us (42%)
  waiting for transfers between devices  162 us (33%)
  matrix products  47.6 us (10%)
  local copies, waits for them, and re-layouts  20.9 us (4%)
  starting transfers between devices  17.7 us (4%)
  other arithmetic  15.4 us (3%)
  between operations  14.5 us (3%)
    all_to_all x2, blocking collectives, on_device(): lax.all_to_all(jnp.stack([flat_part] * lax.axis_size('tp')), 'tp', 0, 0)  83.1 us
    all_gather x1, waiting for transfers between devices, on_device(): shard_rows = lax.all_gather(own_keys, 'seq', axis=0, tiled=True)  75.5 us
    all_to_all x2, blocking collectives, on_device(): lax.all_to_all(sending, 'seq', split_axis=0, concat_axis=0, tiled=True)  72.6 us
    reduce_scatter x2, waiting for transfers between devices, on_device(): lax.psum_scatter(expert_out, 'tp', scatter_dimension=1, tiled=True)  27.8 us
    all_to_all x2, waiting for transfers between devices, on_device(): lax.all_to_all(expert_sum, 'seq', split_axis=0, concat_axis=0, tiled=True)  27.1 us
    all_to_all x2, starting transfers between devices, on_device(): lax.all_to_all(expert_sum, 'seq', split_axis=0, concat_axis=0, tiled=True)  17.5 us
    dot_general x2, matrix products, on_device(): jnp.dot(hidden_units, expert_down[0], preferred_element_type=jnp.float32)  16.7 us
    reduce_scatter x1, waiting for transfers between devices, on_device(): lax.psum_scatter(partial_attention.astype(jnp.bfloat16), 'tp', scatter_di...  16 us
  transfers between devices with their start and end apart: 7, of which 5 were waited for; matrix products, arithmetic and copies ran while one was open for 7% of the time, Pallas kernels for 0%

profile of v1, /device:TPU:32, one launch (start us, length us, event | category | flops | bytes accessed | tf_op | source)
XLA Modules:
  0.0 482.8 jit_solution(4789653768706131129)
XLA Ops:
  9.6 1.9 fusion.82
  12.9 1.8 convolution_convert_fusion.4
  14.7 13.0 %all_gather.12 = bf16[128,1536]{1,0:T(8,128)(2,1)S(1)} all-gather(bf16[128,384]{1,0:T(8,128)(2,1)S(1)} %convolution_convert_fusion.4), channel_id=1, replica_groups=mesh['seq'=64,'tp'=4] {'tp'}, dimensions={1}, use_global_device_ids=true | all-gather | bytes 491520 | tf_op jit(solution)/shard_map/all_gather | solution.py:75
  30.7 15.1 %all-gather.3.cloned.1.call-done = bf16[8,512,256]{2,1,0:T(8,128)(2,1)} async-done(((bf16[2,512,256]{2,1,0:T(8,128)(2,1)}), bf16[8,512,256]{2,1,0:T(8,128)(2,1)}) %all-gather.3.cloned.1.call-update) | async-done | bytes 2097168 | tf_op jit(solution)/shard_map/all_gather | solution.py:72
  45.7 1.7 convolution_bitcast_fusion
  47.5 2.5 copy.151
  50.0 75.5 %all-gather.5.cloned.1.call-done = bf16[2048,576]{1,0:T(8,128)(2,1)} async-done(((bf16[32,576]{1,0:T(8,128)(2,1)}), bf16[2048,576]{1,0:T(8,128)(2,1)}) %all-gather.5.cloned.1.call-update) | async-done | bytes 2359312 | tf_op jit(solution)/shard_map/all_gather | solution.py:93
  125.5 8.8 %select_reduce_fusion = (f32[1024]{0:T(1024)S(1)}, f32[1024,2048]{1,0:T(8,128)}) fusion(s32[2048]{0:T(1024)S(1)} %add.144, s32[2048]{0:T(1024)S(1)} %convert_reduce_fusion, s32[1024]{0:T(1024)S(1)} %le.48, s32[1024]{0:T(1024)S(1)} %eq.54, bf16[2048,576]{1,0:T(8,128)(2,1)} %all-gather.5.cloned.1.call-done, f32[1024,32]{1,0:T(8,128)} %bitcast.159, ...), kind=kOutput, calls=%fused_computation.2 | convolution fusion | flops 2428763136 | bytes 13135872 | tf_op jit(solution)/shard_map/ra,ka->rk/dot_general | solution.py:104
  134.6 5.5 %fusion = f32[1024]{0:T(1024)S(1)} fusion(f32[1024,2048]{1,0:T(8,128)} %get-tuple-element.29, f32[1024]{0:T(1024)S(1)} %broadcast_maximum_fusion, s32[2048]{0:T(1024)S(1)} %add.144, s32[2048]{0:T(1024)S(1)} %convert_reduce_fusion, s32[1024]{0:T(1024)S(1)} %le.48, s32[1024]{0:T(1024)S(1)} %eq.54), kind=kLoop, calls=%fused_computation.4 | loop fusion | flops 12581888 | bytes 8421376 | tf_op jit(solution)/shard_map/reduce_sum | solution.py:108
  140.5 4.3 fusion.10
  144.8 2.4 fusion.8
  148.4 14.0 %all_to_all.35 = f32[4,128,2,130]{1,2,3,0:T(2,128)S(1)} all-to-all(f32[4,128,2,130]{1,2,3,0:T(2,128)S(1)} %maximum_bitcast_fusion), channel_id=1, replica_groups=mesh['seq'=64,'tp'=4] {'tp'}, dimensions={0} | all-to-all | bytes 1064960 | tf_op jit(solution)/shard_map/all_to_all | solution.py:127
  164.4 2.3 reduce-window.19
  168.9 16.0 %reduce-scatter.4.cloned.1.call-done = bf16[128,512]{1,0:T(8,128)(2,1)} async-done(((bf16[128,2048]{1,0:T(8,128)(2,1)}), bf16[128,512]{1,0:T(8,128)(2,1)}) %reduce-scatter.4.cloned.1.call-update) | async-done | bytes 131088 | tf_op jit(solution)/shard_map/reduce_scatter | solution.py:139
  185.9 8.3 %psum.7 = f32[128,1]{0,1:T(1,128)S(1)} all-reduce(f32[128,1]{0,1:T(1,128)S(1)} %bitcast.164), channel_id=1, replica_groups=mesh['seq'=64,'tp'=4] {'tp'}, use_global_device_ids=true, to_apply=%region_16.17 | all-reduce | flops 128 | bytes 1024 | tf_op jit(solution)/shard_map/psum | solution.py:144
  196.3 38.2 %all_to_all.36 = bf16[64,12,512]{2,1,0:T(8,128)(2,1)S(1)} all-to-all(bf16[64,12,512]{2,1,0:T(8,128)(2,1)S(1)} %get-tuple-element.4), channel_id=1, replica_groups=mesh['seq'=64,'tp'=4] {'seq'}, dimensions={0} | all-to-all | bytes 1572864 | tf_op jit(solution)/shard_map/all_to_all | solution.py:169
  235.1 41.5 %all_to_all.37 = bf16[4,768,512]{1,2,0:T(8,128)(2,1)} all-to-all(bf16[4,768,512]{1,2,0:T(8,128)(2,1)S(1)} %stack.6), channel_id=1, replica_groups=mesh['seq'=64,'tp'=4] {'tp'}, dimensions={0} | all-to-all | bytes 6291456 | tf_op jit(solution)/shard_map/all_to_all | solution.py:173
  276.6 4.2 fusion.21
  280.8 8.5 %convolution_convert_fusion.1 = bf16[768,2048]{1,0:T(8,128)(2,1)} fusion(bf16[1,352,2048]{2,1,0:T(8,128)(2,1)} %param.25, bf16[768,2048]{0,1:T(8,128)(2,1)} %bitcast.21, bf16[1,2048,352]{1,2,0:T(8,128)(2,1)} %param.24, f32[768,352]{0,1:T(8,128)} %fusion.21), kind=kOutput, calls=%fused_computation.10 | convolution fusion | flops 2217787392 | bytes 10256384 | tf_op jit(solution)/shard_map/dot_general | solution.py:178
  289.3 34.5 %all_to_all.38 = bf16[64,12,512]{2,1,0:T(8,128)(2,1)S(1)} all-to-all(bf16[64,12,512]{2,1,0:T(8,128)(2,1)S(1)} %get-tuple-element.5), channel_id=1, replica_groups=mesh['seq'=64,'tp'=4] {'seq'}, dimensions={0} | all-to-all | bytes 1572864 | tf_op jit(solution)/shard_map/all_to_all | solution.py:169
  324.4 41.6 %all_to_all.39 = bf16[4,768,512]{1,2,0:T(8,128)(2,1)} all-to-all(bf16[4,768,512]{1,2,0:T(8,128)(2,1)S(1)} %stack.7), channel_id=1, replica_groups=mesh['seq'=64,'tp'=4] {'tp'}, dimensions={0} | all-to-all | bytes 6291456 | tf_op jit(solution)/shard_map/all_to_all | solution.py:173
  366.1 3.2 fusion.23
  369.2 8.2 %convolution_convert_fusion = bf16[768,2048]{1,0:T(8,128)(2,1)} fusion(bf16[1,352,2048]{2,1,0:T(8,128)(2,1)} %param.25, bf16[768,2048]{0,1:T(8,128)(2,1)} %bitcast.27, bf16[1,2048,352]{1,2,0:T(8,128)(2,1)} %param.24, f32[768,352]{0,1:T(8,128)S(1)} %fusion.23), kind=kOutput, calls=%fused_computation.9 | convolution fusion | flops 2217787392 | bytes 10256384 | tf_op jit(solution)/shard_map/dot_general | solution.py:178
  377.5 2.2 reshape.289
  379.7 6.8 %all-to-all-start.3 = ((bf16[64,12,512]{2,1,0:T(8,128)(2,1)}), bf16[64,12,512]{2,1,0:T(8,128)(2,1)S(1)}, u32[]{:S(2)}, u32[]{:S(2)}) async-start(bf16[64,12,512]{2,1,0:T(8,128)(2,1)} %reshape.289), calls=%async_computation.5 | async-start | bytes 2097152 | tf_op jit(solution)/shard_map/all_to_all | solution.py:184
  386.5 27.7 %reduce-scatter.8.cloned.1.call-done = bf16[768,512]{1,0:T(8,128)(2,1)} async-done(((bf16[768,2048]{1,0:T(8,128)(2,1)}), bf16[768,512]{1,0:T(8,128)(2,1)}) %reduce-scatter.8.cloned.1.call-update) | async-done | bytes 786448 | tf_op jit(solution)/shard_map/reduce_scatter | solution.py:181
  414.2 2.1 reshape.292
  416.3 10.7 %all-to-all-start.6 = ((bf16[64,12,512]{2,1,0:T(8,128)(2,1)}), bf16[64,12,512]{2,1,0:T(8,128)(2,1)}, u32[]{:S(2)}, u32[]{:S(2)}) async-start(bf16[64,12,512]{2,1,0:T(8,128)(2,1)} %reshape.292), calls=%async_computation.9 | async-start | bytes 2097152 | tf_op jit(solution)/shard_map/all_to_all | solution.py:184
  427.7 27.1 %all-to-all-done.6 = bf16[64,12,512]{2,1,0:T(8,128)(2,1)} async-done(((bf16[64,12,512]{2,1,0:T(8,128)(2,1)}), bf16[64,12,512]{2,1,0:T(8,128)(2,1)}, u32[]{:S(2)}, u32[]{:S(2)}) %all-to-all-start.6) | async-done | bytes 786464 | tf_op jit(solution)/shard_map/all_to_all | solution.py:184
  454.8 1.7 pad_maximum_fusion
  456.5 2.7 gather_fusion
  461.9 13.4 %all_gather.15 = bf16[128,2048]{1,0:T(8,128)(2,1)S(1)} all-gather(bf16[128,512]{1,0:T(8,128)(2,1)S(1)} %fusion.52), channel_id=1, replica_groups=mesh['seq'=64,'tp'=4] {'tp'}, dimensions={1}, use_global_device_ids=true | all-gather | bytes 655360 | tf_op jit(solution)/shard_map/all_gather | solution.py:196
  (112 shorter events, 20.9 us)
Async XLA Ops:
  7.2 2.4 copy-start
  7.2 4.6 copy-start.11
  7.2 38.6 %all-gather.3.cloned.1.call-start = ((), (), s32[]{:S(2)}) async-start(), calls=%async_computation.10 | async-start | bytes 2621440 | tf_op jit(solution)/shard_map/all_gather | solution.py:72
  7.9 117.6 %all-gather.5.cloned.1.call-start = ((), (), s32[]{:S(2)}) async-start(), calls=%async_computation.11 | async-start | bytes 2662400 | tf_op jit(solution)/shard_map/all_gather | solution.py:93
  9.6 3.3 copy-start.3
  11.9 0.9 copy-start.7
  12.8 172.1 %reduce-scatter.4.cloned.1.call-start = ((), (), s32[]{:S(2)}) async-start(), calls=%async_computation.12 | async-start | bytes 655360 | tf_op jit(solution)/shard_map/reduce_scatter | solution.py:139
  47.5 78.0 %copy-start.8 = (f32[128,8,32]{2,1,0:T(8,128)S(1)}, f32[128,8,32]{2,1,0:T(8,128)}, u32[]{:S(2)}) copy-start(f32[128,8,32]{2,1,0:T(8,128)} %copy.92) | copy-start | bytes 393220
  134.6 5.8 %copy-start.2 = (f32[1024,2048]{1,0:T(8,128)S(1)}, f32[1024,2048]{1,0:T(8,128)}, u32[]{:S(2)}) copy-start(f32[1024,2048]{1,0:T(8,128)} %get-tuple-element.29) | copy-start | bytes 25165828
  140.5 4.3 copy-start.4
  147.6 15.2 %copy-start.6 = (bf16[256,2048]{1,0:T(8,128)(2,1)S(1)}, bf16[256,2048]{1,0:T(8,128)(2,1)}, u32[]{:S(2)}) copy-start(bf16[256,2048]{1,0:T(8,128)(2,1)} %param.19) | copy-start | bytes 3145732
  148.4 15.6 %copy-start.9 = (s32[128,6]{0,1:T(8,128)S(1)}, s32[128,6]{0,1:T(8,128)}, u32[]{:S(2)}) copy-start(s32[128,6]{0,1:T(8,128)} %param.21) | copy-start | bytes 9220
  164.0 213.5 %reduce-scatter.6.cloned.1.call-start = ((), (), s32[]{:S(2)}) async-start(), calls=%async_computation.13 | async-start | bytes 3932160 | tf_op jit(solution)/shard_map/reduce_scatter | solution.py:181
  235.1 41.5 %copy-start.14 = (bf16[1,2048,352]{1,2,0:T(8,128)(2,1)S(1)}, bf16[1,2048,352]{1,2,0:T(8,128)(2,1)}, u32[]{:S(2)}) copy-start(bf16[1,2048,352]{1,2,0:T(8,128)(2,1)} %param.23) | copy-start | bytes 4325380
  289.2 125.0 %reduce-scatter.8.cloned.1.call-start = ((), (), s32[]{:S(2)}) async-start(), calls=%async_computation.14 | async-start | bytes 3932160 | tf_op jit(solution)/shard_map/reduce_scatter | solution.py:181
  324.4 41.7 %copy-start.15 = (bf16[1,2048,352]{1,2,0:T(8,128)(2,1)S(1)}, bf16[1,2048,352]{1,2,0:T(8,128)(2,1)}, u32[]{:S(2)}) copy-start(bf16[1,2048,352]{1,2,0:T(8,128)(2,1)} %param.23) | copy-start | bytes 4325380
  379.7 36.7 %all-to-all-start.3 = ((bf16[64,12,512]{2,1,0:T(8,128)(2,1)}), bf16[64,12,512]{2,1,0:T(8,128)(2,1)S(1)}, u32[]{:S(2)}, u32[]{:S(2)}) async-start(bf16[64,12,512]{2,1,0:T(8,128)(2,1)} %reshape.289), calls=%async_computation.5 | async-start | bytes 2097152 | tf_op jit(solution)/shard_map/all_to_all | solution.py:184
  386.5 40.7 %copy-start.10 = (f32[128,6]{0,1:T(8,128)S(1)}, f32[128,6]{0,1:T(8,128)}, u32[]{:S(2)}) copy-start(f32[128,6]{0,1:T(8,128)} %param.22) | copy-start | bytes 9220
  416.3 38.5 %all-to-all-start.6 = ((bf16[64,12,512]{2,1,0:T(8,128)(2,1)}), bf16[64,12,512]{2,1,0:T(8,128)(2,1)}, u32[]{:S(2)}, u32[]{:S(2)}) async-start(bf16[64,12,512]{2,1,0:T(8,128)(2,1)} %reshape.292), calls=%async_computation.9 | async-start | bytes 2097152 | tf_op jit(solution)/shard_map/all_to_all | solution.py:184
  459.2 1.5 copy-start.5
  459.5 1.2 copy-start.12
  459.5 1.2 copy-start.13
  459.5 16.6 %copy-start.1 = (bf16[2048,576]{0,1:T(8,128)(2,1)S(1)}, bf16[2048,576]{0,1:T(8,128)(2,1)}, u32[]{:S(2)}) copy-start(bf16[2048,576]{0,1:T(8,128)(2,1)} %param.16) | copy-start | bytes 7077892
Sparse Core Ops, SparseCore 0:
  9.8 35.8 all-gather.2
  48.5 76.9 all-gather.4
  164.1 20.7 reduce-scatter.3
  289.4 36.5 reduce-scatter.5
  377.6 36.5 reduce-scatter.7
